TPU v7x, 256 devices: a whole 4x4x8 slice. The times are simulated.
256 devices in a mesh: ctx: 64 (over z, y, core), hg: 4 (over x).
Axes of the slice: x: 4, y: 4, z: 8, core: 2. Of those that a mesh axis runs over, the one named last changes fastest.
Arguments:
- doc_ids: int32 [32768], P('ctx'), may hold values from 0 to 63, never falling along the last dimension, each value on 1 to 1024 neighbouring positions
- rotated_queries: bfloat16 [32768, 2048], P('ctx', 'hg'), may hold values from -6 to 6
- rotated_keys: bfloat16 [32768, 512], P('ctx', 'hg'), may hold values from -6 to 6
- value_matrix: bfloat16 [32768, 512], P('ctx', 'hg'), may hold values from -6 to 6
- out_proj: bfloat16 [4096, 2048], P('ctx', 'hg'), may hold values from -0.125 to 0.125
- cotangent: bfloat16 [32768, 4096], P('ctx'), may hold values from -16 to 16
Outputs:
- layer_output: bfloat16 [32768, 4096], P('ctx', 'hg')
- query_grad: bfloat16 [32768, 2048], P('ctx', 'hg')
- key_gradient: bfloat16 [32768, 512], P('ctx', 'hg')
- value_gradient: bfloat16 [32768, 512], P('ctx', 'hg')
- proj_grad: bfloat16 [4096, 2048], P('ctx', 'hg')
Inputs may be any that keep to these rules, and one draw needn't show every extreme that they name: `doc_ids`: document ids in token order, never falling; every document has 1 to 1024 tokens and one has exactly 1024.
All inputs are finite; a program needn't handle non-finite values.
Results may differ from a plain program's by a relative error of at most 0.013.
Values may be sent and summed in bfloat16 or wider, within the bound.
A program may use at most 128 MiB of HBM per device.

v0:
```python
import jax
import jax.numpy as jnp
from jax import lax
from jax.sharding import PartitionSpec as P

HEAD_SIZE = 128
TOK_DEV = 512
DOC_MOST = 1024


def from_behind(value, axis, by):
    devices = lax.axis_size(axis)
    pairs = [(i, i + by) for i in range(devices) if 0 <= i + by < devices]
    return lax.ppermute(value, axis, pairs)


def contract_last(left_side, right_side):
    return lax.dot_general(
        left_side, right_side, (((1,), (1,)), ((), ())), preferred_element_type=jnp.float32
    )


def contract_first(left_side, right_side):
    return lax.dot_general(
        left_side, right_side, (((0,), (0,)), ((), ())), preferred_element_type=jnp.float32
    )


def body(doc_ids, rotated_queries, rotated_keys, value_matrix, out_proj, cotangent):
    row_count = rotated_queries.shape[0]
    head_count = rotated_queries.shape[1] // HEAD_SIZE
    kv_count = rotated_keys.shape[1] // HEAD_SIZE
    group_length = head_count // kv_count
    steps_back = DOC_MOST // TOK_DEV
    score_scale = HEAD_SIZE ** (-0.5)
    device_index = lax.axis_index("ctx")
    earlier = [(rotated_keys, value_matrix, doc_ids)]
    for offset in range(1, steps_back + 1):
        earlier.append(from_behind((rotated_keys, value_matrix, doc_ids), "ctx", offset))
    ordered = earlier[::-1]
    key_cat = jnp.concatenate([member[0] for member in ordered], 0)
    value_cat = jnp.concatenate([member[1] for member in ordered], 0)
    doc_cat = jnp.concatenate([member[2] for member in ordered], 0)
    key_width = key_cat.shape[0]
    query_pos = jnp.arange(row_count, dtype=jnp.int32)
    column_pos = jnp.arange(key_width, dtype=jnp.int32)
    key_pos = column_pos - steps_back * row_count
    first_valid = (steps_back - device_index) * row_count
    allowed = (
        (doc_ids[:, None] == doc_cat[None, :])
        & (key_pos[None, :] <= query_pos[:, None])
        & (column_pos[None, :] >= first_valid)
    )
    outputs = []
    probs_list = []
    for head_index in range(head_count):
        kv_index = head_index // group_length
        query_head = rotated_queries[:, head_index * HEAD_SIZE : (head_index + 1) * HEAD_SIZE]
        key_head = key_cat
        value_head = value_cat
        scores = contract_last(query_head, key_head) * score_scale
        masked = jnp.where(allowed, scores, -jnp.inf)
        row_max = jnp.max(masked, axis=1, keepdims=True)
        row_sum = jnp.sum(jnp.where(allowed, jnp.exp(masked - row_max), 0.0), axis=1, keepdims=True)
        log_total = row_max + jnp.log(row_sum)
        weights = jnp.where(allowed, jnp.exp(masked - log_total), 0.0).astype(jnp.bfloat16)
        probs_list.append(weights)
        outputs.append(
            jnp.dot(weights, value_head, preferred_element_type=jnp.float32).astype(jnp.bfloat16)
        )
    attended = jnp.concatenate(outputs, 1)
    partial_value = contract_last(attended, lax.all_gather(out_proj, "ctx", axis=0, tiled=True))
    layer_output = lax.psum_scatter(
        partial_value.astype(jnp.bfloat16), "hg", scatter_dimension=1, tiled=True
    )
    columns = cotangent
    attention_gradient = jnp.dot(
        columns,
        lax.all_gather(out_proj, "ctx", axis=0, tiled=True),
        preferred_element_type=jnp.float32,
    ).astype(jnp.bfloat16)
    columns = cotangent
    proj_grad = lax.psum_scatter(
        contract_first(columns, attended), "ctx", scatter_dimension=0, tiled=True
    ).astype(jnp.bfloat16)
    key_parts = [jnp.zeros((key_width, HEAD_SIZE), jnp.float32)]
    value_parts = [jnp.zeros((key_width, HEAD_SIZE), jnp.float32)]
    query_grads = []
    for head_index in range(head_count):
        kv_index = head_index // group_length
        query_head = rotated_queries[:, head_index * HEAD_SIZE : (head_index + 1) * HEAD_SIZE]
        key_head = key_cat
        value_head = value_cat
        grad_head = attention_gradient[:, head_index * HEAD_SIZE : (head_index + 1) * HEAD_SIZE]
        weights = probs_list[head_index]
        row_delta = jnp.sum(
            grad_head.astype(jnp.float32) * outputs[head_index].astype(jnp.float32),
            axis=1,
            keepdims=True,
        )
        grad_dots = contract_last(grad_head, value_head)
        shifted = (weights.astype(jnp.float32) * (grad_dots - row_delta) * score_scale).astype(
            jnp.bfloat16
        )
        query_grads.append(
            jnp.dot(shifted, key_head, preferred_element_type=jnp.float32).astype(jnp.bfloat16)
        )
        key_parts[kv_index] = key_parts[kv_index] + contract_first(shifted, query_head)
        value_parts[kv_index] = value_parts[kv_index] + contract_first(weights, grad_head)
    query_grad = jnp.concatenate(query_grads, 1)
    key_all = key_parts[0]
    value_all = value_parts[0]
    pieces = []
    for offset in range(steps_back + 1):
        lower = (steps_back - offset) * row_count
        pieces.append((key_all[lower : lower + row_count], value_all[lower : lower + row_count]))
    key_sum, value_sum = pieces[0]
    for offset in range(1, steps_back + 1):
        arrived = (
            from_behind(pieces[offset][0].astype(jnp.bfloat16), "ctx", -offset).astype(jnp.float32),
            from_behind(pieces[offset][1].astype(jnp.bfloat16), "ctx", -offset).astype(jnp.float32),
        )
        key_sum = key_sum + arrived[0]
        value_sum = value_sum + arrived[1]
    key_gradient = key_sum.astype(jnp.bfloat16)
    value_gradient = value_sum.astype(jnp.bfloat16)
    return (layer_output, query_grad, key_gradient, value_gradient, proj_grad)


def solution(mesh):
    in_specs = (
        P("ctx"),
        P("ctx", "hg"),
        P("ctx", "hg"),
        P("ctx", "hg"),
        P("ctx", "hg"),
        P("ctx", None),
    )
    out_specs = (P("ctx", "hg"), P("ctx", "hg"), P("ctx", "hg"), P("ctx", "hg"), P("ctx", "hg"))
    return jax.shard_map(body, mesh=mesh, in_specs=in_specs, out_specs=out_specs, check_vma=False)
```

profile of v0, /device:TPU:1, one launch (start us, length us, event | category | flops | bytes accessed | tf_op | source)
XLA Modules:
  0.0 323.6 jit_solution(5322077553955381528)
XLA Ops:
  7.2 0.7 all-gather.2.cloned.1.call-update
  7.9 4.0 %collective-permute-start.2 = (bf16[512,128]{1,0:T(8,128)(2,1)}, bf16[512,128]{1,0:T(8,128)(2,1)S(1)}, u32[]{:S(2)}, u32[]{:S(2)}) collective-permute-start(bf16[512,128]{1,0:T(8,128)(2,1)} %param.8), channel_id=1, source_target_pairs={{0,8},{4,12},{8,16},{12,20},{16,24},{20,28},{24,32},{28,36},{32,40... | collective-permute-start | bytes 393224 | tf_op jit(solution)/shard_map/ppermute | solution.py:14
  12.0 4.0 %collective-permute-start.3 = (bf16[512,128]{1,0:T(8,128)(2,1)}, bf16[512,128]{1,0:T(8,128)(2,1)S(1)}, u32[]{:S(2)}, u32[]{:S(2)}) collective-permute-start(bf16[512,128]{1,0:T(8,128)(2,1)} %param.8), channel_id=1, source_target_pairs={{0,4},{4,8},{8,12},{12,16},{16,20},{20,24},{24,28},{28,32},{32,36}... | collective-permute-start | bytes 393224 | tf_op jit(solution)/shard_map/ppermute | solution.py:14
  16.0 1.9 collective-permute-start.1
  18.0 2.9 collective-permute-start
  20.9 3.2 collective-permute-start.4
  24.1 4.1 %collective-permute-start.5 = (bf16[512,128]{1,0:T(8,128)(2,1)}, bf16[512,128]{1,0:T(8,128)(2,1)S(1)}, u32[]{:S(2)}, u32[]{:S(2)}) collective-permute-start(bf16[512,128]{1,0:T(8,128)(2,1)} %param.9), channel_id=1, source_target_pairs={{0,4},{4,8},{8,12},{12,16},{16,20},{20,24},{24,28},{28,32},{32,36}... | collective-permute-start | bytes 393224 | tf_op jit(solution)/shard_map/ppermute | solution.py:14
  28.3 0.7 pad_add_fusion
  29.1 0.9 constant_dynamic-update-slice_fusion
  30.6 0.9 constant_dynamic-update-slice_fusion.3
  31.5 2.2 fusion.48
  33.8 1.2 fusion.49
  35.0 1.2 fusion.50
  36.1 1.2 fusion.51
  37.3 3.6 %select_reduce_fusion.3 = (f32[512]{0:T(512)S(1)}, f32[512]{0:T(512)S(1)}, f32[512]{0:T(512)S(1)}, f32[512]{0:T(512)S(1)}) fusion(f32[512,1536]{0,1:T(8,128)S(1)} %get-tuple-element.32, f32[512]{0:T(512)S(1)} %get-tuple-element.31, pred[1536]{0:T(1024)(128)(4,1)S(1)} %iota_compare_fusion.1, s32[1536]{0:T(1024)S(1)} %iota_add_fusion, ...), kind=kLoop, calls=%fused_computation.33 | loop fusion | flops 12580864 | bytes 12615168 | tf_op jit(solution)/shard_map/reduce_sum | solution.py:64
  40.9 4.0 %select_convert_fusion.3 = (bf16[512,1536]{0,1:T(8,128)(2,1)}, bf16[512,1536]{0,1:T(8,128)(2,1)S(1)}, bf16[512,1536]{0,1:T(8,128)(2,1)S(1)}, bf16[512,1536]{0,1:T(8,128)(2,1)S(1)}) fusion(f32[512,1536]{0,1:T(8,128)S(1)} %get-tuple-element.32, f32[512]{0:T(512)S(1)} %get-tuple-element.47, pred[1536]{0:T(1024)(128)(4,1)S(1)} %iota_compare_fusion.1, ...), kind=kLoop, calls=%fused_computation.32 | loop fusion | flops 12582912 | bytes 18898432 | tf_op jit(solution)/shard_map/convert_element_type | solution.py:66
  46.5 47.7 %all-gather.2.cloned.1.call-done = bf16[4096,512]{1,0:T(8,128)(2,1)} async-done(((bf16[64,512]{1,0:T(8,128)(2,1)}), bf16[4096,512]{1,0:T(8,128)(2,1)}) %all-gather.2.cloned.1.call-update) | async-done | bytes 4194320 | tf_op jit(solution)/shard_map/all_gather | solution.py:72
  94.2 6.0 %convolution_convert_fusion.1 = bf16[512,512]{0,1:T(8,128)(2,1)S(1)} fusion(bf16[512,4096]{1,0:T(8,128)(2,1)} %param.11, bf16[4096,512]{1,0:T(8,128)(2,1)} %all-gather.2.cloned.1.call-done), kind=kOutput, calls=%fused_computation.47 | convolution fusion | flops 2147745792 | bytes 8912896 | tf_op jit(solution)/shard_map/dot_general | solution.py:77
  101.0 0.7 copy-done.18
  101.6 1.0 copy-done.6
  102.6 5.6 %convolution_bitcast_fusion = f32[4096,512]{0,1:T(8,128)} fusion(bf16[512,4096]{1,0:T(8,128)(2,1)S(1)} %copy-done.6, bf16[512,128]{0,1:T(8,128)(2,1)S(1)} %convolution_convert_fusion.6, bf16[512,128]{0,1:T(8,128)(2,1)S(1)} %convolution_convert_fusion.7, bf16[512,128]{0,1:T(8,128)(2,1)S(1)} %convolution_convert_fusion.8, bf16[512,128]{0,1:T(8,128)(2,1)S(1)} %get-tuple-element.39), kind=kOutput, calls=%fused_computation | convolution fusion | flops 2149580800 | bytes 13107200 | tf_op jit(solution)/shard_map/dot_general | solution.py:24
  108.2 9.0 %copy.27 = f32[4096,512]{1,0:T(8,128)} copy(f32[4096,512]{0,1:T(8,128)} %convolution_bitcast_fusion) | data formatting | bytes 16777216
  117.6 6.6 %convolution_convert_fusion = bf16[512,4096]{1,0:T(8,128)(2,1)} fusion(bf16[4096,512]{1,0:T(8,128)(2,1)} %all-gather.2.cloned.1.call-done, bf16[512,128]{0,1:T(8,128)(2,1)S(1)} %convolution_convert_fusion.6, bf16[512,128]{0,1:T(8,128)(2,1)S(1)} %convolution_convert_fusion.7, bf16[512,128]{0,1:T(8,128)(2,1)S(1)} %convolution_convert_fusion.8, ...), kind=kOutput, calls=%fused_computation.1 | convolution fusion | flops 2151677952 | bytes 8912896 | tf_op jit(solution)/shard_map/dot_general | solution.py:18
  124.2 1.7 fusion.18
  126.0 1.2 copy-done.7
  127.6 0.6 fusion.19
  128.3 1.1 copy-done.9
  129.8 0.6 fusion.20
  131.3 0.6 fusion.21
  131.9 1.2 copy-done.12
  133.5 0.8 pad_maximum_fusion.1
  134.4 2.1 copy.21
  136.4 2.2 fusion.32
  138.6 2.1 convolution_add_fusion.5
  141.4 0.6 fusion.52
  142.0 1.3 collective-permute-start.7
  143.3 2.2 collective-permute-start.6
  146.6 0.6 convolution_add_fusion.1
  147.8 1.3 collective-permute-start.9
  149.1 1.9 collective-permute-start.8
  151.1 0.7 fusion.25
  151.8 4.2 %collective-permute-done.9 = bf16[512,128]{1,0:T(8,128)(2,1)S(1)} collective-permute-done((bf16[512,128]{1,0:T(8,128)(2,1)S(1)}, bf16[512,128]{1,0:T(8,128)(2,1)S(1)}, u32[]{:S(2)}, u32[]{:S(2)}) %collective-permute-start.9) | collective-permute-done | bytes 131104 | tf_op jit(solution)/shard_map/ppermute | solution.py:14
  155.9 1.3 collective-permute-done.8
  157.2 0.7 fusion.23
  157.9 103.7 %reduce-scatter.7.cloned.1.call-done = f32[64,512]{1,0:T(8,128)} async-done(((f32[4096,512]{1,0:T(8,128)}), f32[64,512]{1,0:T(8,128)}) %reduce-scatter.7.cloned.1.call-update) | async-done | bytes 131088
  261.6 1.0 copy.28
  262.7 0.7 copy.22
  263.4 53.7 %reduce-scatter.5.cloned.1.call-done = bf16[512,1024]{1,0:T(8,128)(2,1)} async-done(((bf16[512,4096]{1,0:T(8,128)(2,1)}), bf16[512,1024]{1,0:T(8,128)(2,1)}) %reduce-scatter.5.cloned.1.call-update) | async-done | bytes 1048592 | tf_op jit(solution)/shard_map/reduce_scatter | solution.py:73
  (80 shorter events, 7.8 us)
Async XLA Ops:
  7.2 87.0 %all-gather.2.cloned.1.call-start = ((), (), s32[]{:S(2)}) async-start(), calls=%async_computation.2 | async-start | bytes 4259840 | tf_op jit(solution)/shard_map/all_gather | solution.py:72
  7.9 253.8 %reduce-scatter.7.cloned.1.call-start = ((), (), s32[]{:S(2)}) async-start(), calls=%async_computation.4 | async-start | bytes 8519680
  7.9 21.1 %collective-permute-start.2 = (bf16[512,128]{1,0:T(8,128)(2,1)}, bf16[512,128]{1,0:T(8,128)(2,1)S(1)}, u32[]{:S(2)}, u32[]{:S(2)}) collective-permute-start(bf16[512,128]{1,0:T(8,128)(2,1)} %param.8), channel_id=1, source_target_pairs={{0,8},{4,12},{8,16},{12,20},{16,24},{20,28},{24,32},{28,36},{32,40... | collective-permute-start | bytes 393224 | tf_op jit(solution)/shard_map/ppermute | solution.py:14
  12.0 17.0 %collective-permute-start.3 = (bf16[512,128]{1,0:T(8,128)(2,1)}, bf16[512,128]{1,0:T(8,128)(2,1)S(1)}, u32[]{:S(2)}, u32[]{:S(2)}) collective-permute-start(bf16[512,128]{1,0:T(8,128)(2,1)} %param.8), channel_id=1, source_target_pairs={{0,4},{4,8},{8,12},{12,16},{16,20},{20,24},{24,28},{28,32},{32,36}... | collective-permute-start | bytes 393224 | tf_op jit(solution)/shard_map/ppermute | solution.py:14
  16.0 8.1 %collective-permute-start.1 = (s32[512]{0:T(512)}, s32[512]{0:T(512)S(1)}, u32[]{:S(2)}, u32[]{:S(2)}) collective-permute-start(s32[512]{0:T(512)} %param.6), channel_id=1, source_target_pairs={{0,4},{4,8},{8,12},{12,16},{16,20},{20,24},{24,28},{28,32},{32,36}... | collective-permute-start | bytes 6152 | tf_op jit(solution)/shard_map/ppermute | solution.py:14
  18.0 10.3 %collective-permute-start = (s32[512]{0:T(512)}, s32[512]{0:T(512)S(1)}, u32[]{:S(2)}, u32[]{:S(2)}) collective-permute-start(s32[512]{0:T(512)} %param.6), channel_id=1, source_target_pairs={{0,8},{4,12},{8,16},{12,20},{16,24},{20,28},{24,32},{28,36},{32,40... | collective-permute-start | bytes 6152 | tf_op jit(solution)/shard_map/ppermute | solution.py:14
  20.9 9.1 %collective-permute-start.4 = (bf16[512,128]{1,0:T(8,128)(2,1)}, bf16[512,128]{1,0:T(8,128)(2,1)S(1)}, u32[]{:S(2)}, u32[]{:S(2)}) collective-permute-start(bf16[512,128]{1,0:T(8,128)(2,1)} %param.9), channel_id=1, source_target_pairs={{0,8},{4,12},{8,16},{12,20},{16,24},{20,28},{24,32},{28,36},{32,40... | collective-permute-start | bytes 393224 | tf_op jit(solution)/shard_map/ppermute | solution.py:14
  24.1 6.4 %collective-permute-start.5 = (bf16[512,128]{1,0:T(8,128)(2,1)}, bf16[512,128]{1,0:T(8,128)(2,1)S(1)}, u32[]{:S(2)}, u32[]{:S(2)}) collective-permute-start(bf16[512,128]{1,0:T(8,128)(2,1)} %param.9), channel_id=1, source_target_pairs={{0,4},{4,8},{8,12},{12,16},{16,20},{20,24},{24,28},{28,32},{32,36}... | collective-permute-start | bytes 393224 | tf_op jit(solution)/shard_map/ppermute | solution.py:14
  30.0 6.2 %copy-start.19 = (bf16[1536,128]{1,0:T(8,128)(2,1)}, bf16[1536,128]{1,0:T(8,128)(2,1)S(1)}, u32[]{:S(2)}) copy-start(bf16[1536,128]{1,0:T(8,128)(2,1)S(1)} %constant_dynamic-update-slice_fusion) | copy-start | bytes 1179652
  31.5 14.3 %copy-start.21 = (bf16[1536,128]{1,0:T(8,128)(2,1)}, bf16[1536,128]{1,0:T(8,128)(2,1)S(1)}, u32[]{:S(2)}) copy-start(bf16[1536,128]{1,0:T(8,128)(2,1)S(1)} %constant_dynamic-update-slice_fusion.3) | copy-start | bytes 1179652
  31.5 2.3 copy-start.13
  31.5 2.3 copy-start.24
  44.9 1.2 copy-start
  94.2 6.0 %copy-start.3 = (bf16[512,1536]{0,1:T(8,128)(2,1)S(1)}, bf16[512,1536]{0,1:T(8,128)(2,1)}, u32[]{:S(2)}) copy-start(bf16[512,1536]{0,1:T(8,128)(2,1)} %get-tuple-element.27) | copy-start | bytes 4718596
  94.2 6.0 %copy-start.22 = (bf16[1536,128]{1,0:T(8,128)(2,1)S(1)}, bf16[1536,128]{1,0:T(8,128)(2,1)}, u32[]{:S(2)}) copy-start(bf16[1536,128]{1,0:T(8,128)(2,1)} %copy-done.21) | copy-start | bytes 1179652
  100.2 0.8 copy-start.15
  100.2 2.4 copy-start.6
  100.9 0.7 copy-start.18
  117.3 199.8 %reduce-scatter.5.cloned.1.call-start = ((), (), s32[]{:S(2)}) async-start(), calls=%async_computation.3 | async-start | bytes 5242880 | tf_op jit(solution)/shard_map/reduce_scatter | solution.py:73
  124.2 3.0 copy-start.20
  124.2 3.4 %copy-start.16 = (bf16[512,512]{0,1:T(8,128)(2,1)S(1)}, bf16[512,512]{0,1:T(8,128)(2,1)}, u32[]{:S(2)}) copy-start(bf16[512,512]{0,1:T(8,128)(2,1)} %copy-done.15) | copy-start | bytes 1572868
  124.2 3.4 %copy-start.23 = (bf16[1536,128]{1,0:T(8,128)(2,1)S(1)}, bf16[1536,128]{1,0:T(8,128)(2,1)}, u32[]{:S(2)}) copy-start(bf16[1536,128]{1,0:T(8,128)(2,1)} %copy-done.21) | copy-start | bytes 1179652
  126.0 1.2 copy-start.7
  127.6 2.2 copy-start.1
  128.2 1.1 copy-start.9
  129.8 1.5 copy-start.4
  130.5 3.0 copy-start.11
  131.9 1.2 copy-start.12
  136.4 4.3 %copy-start.10 = (bf16[512,1536]{0,1:T(8,128)(2,1)S(1)}, bf16[512,1536]{0,1:T(8,128)(2,1)}, u32[]{:S(2)}) copy-start(bf16[512,1536]{0,1:T(8,128)(2,1)} %copy-done.9) | copy-start | bytes 4718596
  136.4 4.3 %copy-start.14 = (bf16[512,512]{1,0:T(8,128)(2,1)S(1)}, bf16[512,512]{1,0:T(8,128)(2,1)}, u32[]{:S(2)}) copy-start(bf16[512,512]{1,0:T(8,128)(2,1)} %param.7) | copy-start | bytes 1572868
  138.6 2.8 copy-start.8
  140.8 4.7 %copy-start.5 = (bf16[512,1536]{0,1:T(8,128)(2,1)S(1)}, bf16[512,1536]{0,1:T(8,128)(2,1)}, u32[]{:S(2)}) copy-start(bf16[512,1536]{0,1:T(8,128)(2,1)} %get-tuple-element.27) | copy-start | bytes 4718596
  140.8 4.7 %copy-start.17 = (bf16[512,512]{0,1:T(8,128)(2,1)S(1)}, bf16[512,512]{0,1:T(8,128)(2,1)}, u32[]{:S(2)}) copy-start(bf16[512,512]{0,1:T(8,128)(2,1)} %copy-done.15) | copy-start | bytes 1572868
  141.4 4.7 %copy-start.2 = (bf16[512,1536]{0,1:T(8,128)(2,1)S(1)}, bf16[512,1536]{0,1:T(8,128)(2,1)}, u32[]{:S(2)}) copy-start(bf16[512,1536]{0,1:T(8,128)(2,1)} %copy-done) | copy-start | bytes 4718596
  142.0 9.0 %collective-permute-start.7 = (bf16[512,128]{1,0:T(8,128)(2,1)S(1)}, bf16[512,128]{1,0:T(8,128)(2,1)S(1)}, u32[]{:S(2)}, u32[]{:S(2)}) collective-permute-start(bf16[512,128]{1,0:T(8,128)(2,1)S(1)} %get-tuple-element.26), channel_id=1, source_target_pairs={{8,0},{12,4},{16,8},{20,12},{24,16},{28,20},{32,24},{36,28},{40,32... | collective-permute-start | bytes 393224 | tf_op jit(solution)/shard_map/ppermute | solution.py:14
  143.3 7.8 %collective-permute-start.6 = (bf16[512,128]{1,0:T(8,128)(2,1)S(1)}, bf16[512,128]{1,0:T(8,128)(2,1)S(1)}, u32[]{:S(2)}, u32[]{:S(2)}) collective-permute-start(bf16[512,128]{1,0:T(8,128)(2,1)S(1)} %get-tuple-element.25), channel_id=1, source_target_pairs={{4,0},{8,4},{12,8},{16,12},{20,16},{24,20},{28,24},{32,28},{36,32}... | collective-permute-start | bytes 393224 | tf_op jit(solution)/shard_map/ppermute | solution.py:14
  147.8 8.1 %collective-permute-start.9 = (bf16[512,128]{1,0:T(8,128)(2,1)S(1)}, bf16[512,128]{1,0:T(8,128)(2,1)S(1)}, u32[]{:S(2)}, u32[]{:S(2)}) collective-permute-start(bf16[512,128]{1,0:T(8,128)(2,1)S(1)} %get-tuple-element.24), channel_id=1, source_target_pairs={{8,0},{12,4},{16,8},{20,12},{24,16},{28,20},{32,24},{36,28},{40,32... | collective-permute-start | bytes 393224 | tf_op jit(solution)/shard_map/ppermute | solution.py:14
  149.1 8.1 %collective-permute-start.8 = (bf16[512,128]{1,0:T(8,128)(2,1)S(1)}, bf16[512,128]{1,0:T(8,128)(2,1)S(1)}, u32[]{:S(2)}, u32[]{:S(2)}) collective-permute-start(bf16[512,128]{1,0:T(8,128)(2,1)S(1)} %get-tuple-element.23), channel_id=1, source_target_pairs={{4,0},{8,4},{12,8},{16,12},{20,16},{24,20},{28,24},{32,28},{36,32}... | collective-permute-start | bytes 393224 | tf_op jit(solution)/shard_map/ppermute | solution.py:14
Sparse Core Ops, SparseCore 0:
  10.7 83.4 all-gather.1
  117.4 144.2 reduce-scatter.6
  264.8 52.2 reduce-scatter.4
where the time goes:
time: 324 us
  waiting for transfers between devices  212 us (65%)
  matrix products  38.7 us (12%)
  starting transfers between devices  27.3 us (8%)
  local copies, waits for them, and re-layouts  20.9 us (6%)
  between operations  14.4 us (4%)
  other arithmetic  10.5 us (3%)
    unnamed x4, waiting for transfers between devices  104 us
    reduce_scatter x1, waiting for transfers between devices, body(): lax.psum_scatter(partial_value.astype(jnp.bfloat16), 'hg', scatter_dimens...  53.7 us
    all_gather x1, waiting for transfers between devices, body(): lax.all_gather(out_proj, 'ctx', axis=0, tiled=True)  47.7 us
    ppermute x10, starting transfers between devices, from_behind(): return lax.ppermute(value, axis, pairs)  26.9 us
    unnamed x58, local copies, waits for them, and re-layouts  19 us
    dot_general x9, matrix products, contract_last(): lax.dot_general(left_side, right_side, (((1,), (1,)), ((), ())), preferre...  16 us
    dot_general x9, matrix products, contract_first(): lax.dot_general(left_side, right_side, (((0,), (0,)), ((), ())), preferre...  13.3 us
  transfers between devices with their start and end apart: 13, of which 6 were waited for; matrix products, arithmetic and copies ran while one was open for 13% of the time, Pallas kernels for 0%

commit v1 on v0

v1 whole, which is shorter than its diff:
```python
import jax
import jax.numpy as jnp
from jax import lax
from jax.experimental import pallas as pl
from jax.experimental.pallas import tpu as pltpu
from jax.sharding import PartitionSpec as P

MESH = pl.DeviceIdType.MESH
BF = jnp.bfloat16
F32 = jnp.float32
I32 = jnp.int32
DMA = pltpu.SemaphoreType.DMA

HEAD = 128
HEADS = 4
TOK = 512
QB = 256
KW = 1280
WIN = 1536
NX, NY, NZ = 4, 4, 8
CTX = 64
SCALE = HEAD ** (-0.5)
EXP_SCALE = SCALE * 1.4426950408889634
MASKED = -1e30


def nn(a, b):
    return jnp.dot(a, b, preferred_element_type=F32)


def nt(a, b):
    return lax.dot_general(a, b, (((1,), (1,)), ((), ())), preferred_element_type=F32)


def al(value, by):
    return pl.multiple_of(value, by)


def kernel(
    doc_ref, q_ref, k_ref, v_ref, w_ref, cot_hbm,
    out_ref, qg_ref, kg_ref, vg_ref, pg_ref,
    cot, kwin, vwin, dwin, kt, vt, wall, st_ref, pbuf, dsbuf, att_t, att, inv_l, d_o, dos, qs, dk, dv,
    gbuf, drecv, gh, yr1, yr2, yh, zr, fts, frec, lbuf, xr1, xr2, gks, gkr,
    cot_sem, hs, hr, zs_w, zr_w, ys_w, yr_w, rs_w, rr_w, ps_w, pr_w,
    ds_s, dr_s, y1s, y1r, y2s, y2r, zs_g, zr_g, fs, fr, x1s, x1r, x2s, x2r, gs, gr,
):
    c = lax.axis_index("ctx")
    x = lax.axis_index("hg")
    z = lax.div(c, 8)
    y = lax.rem(lax.div(c, 2), NY)
    k = lax.rem(c, 2)

    def at_ctx(by):
        return (lax.rem(c + by + CTX, CTX), x)

    def at_z(by):
        return (lax.rem(z + by, NZ) * 8 + y * 2 + k, x)

    def at_y(by):
        return (z * 8 + lax.rem(y + by, NY) * 2 + k, x)

    def at_x(by):
        return (c, lax.rem(x + by, NX))

    partner = (z * 8 + y * 2 + (1 - k), x)

    def rcopy(src, dst, send, recv, device):
        return pltpu.make_async_remote_copy(
            src_ref=src, dst_ref=dst, send_sem=send, recv_sem=recv,
            device_id=device, device_id_type=MESH,
        )

    cot_copy = pltpu.make_async_copy(cot_hbm, cot, cot_sem)
    cot_copy.start()

    barrier = pltpu.get_barrier_semaphore()
    peers = [partner, at_y(1), at_y(3), at_x(1), at_x(3), at_ctx(1), at_ctx(2), at_ctx(-1), at_ctx(-2)]
    peers += [at_z(d) for d in range(1, NZ)]
    for peer in peers:
        pl.semaphore_signal(barrier, inc=1, device_id=peer, device_id_type=MESH)
    pl.semaphore_wait(barrier, len(peers))

    own_parts = ((doc_ref, dwin, 0), (k_ref, kwin, 1), (v_ref, vwin, 2))

    def piece(ref, index, at):
        return ref.at[at] if index == 0 else ref.at[pl.ds(at * TOK, TOK)]

    def halo_next(i):
        mine, ref, n = own_parts[i]
        return rcopy(mine, piece(ref, n, 1), hs.at[0, n], hr.at[1, n], at_ctx(1))

    def halo_far(i):
        mine, ref, n = own_parts[i]
        return rcopy(mine, piece(ref, n, 0), hs.at[1, n], hr.at[0, n], at_ctx(2))

    def halo_relay(i):
        _, ref, n = own_parts[i]
        return rcopy(piece(ref, n, 1), piece(ref, n, 0), hs.at[2, n], hr.at[0, n], partner)

    for i in range(3):
        halo_next(i).start()

        @pl.when(k == 0)
        def _():
            halo_far(i).start()

    def half_rows(a):
        return pl.ds(32 * a, 32)

    def gather_z(a, d):
        return rcopy(
            w_ref.at[half_rows(a)], wall.at[z, y, k, half_rows(a)], zs_w.at[a, d], zr_w.at[a, d], at_z(d)
        )

    def slab(yy, a):
        return wall.at[:, yy, k, half_rows(a)]

    def gather_y(a, side):
        return rcopy(slab(y, a), slab(y, a), ys_w.at[a, side], yr_w.at[a, side], at_y(1 if side == 0 else 3))

    def gather_relay(a, side):
        src = wall.at[pl.ds(4 * side, 4), lax.rem(y + (3 if side == 0 else 1), NY), k, half_rows(a)]
        return rcopy(src, src, rs_w.at[a, side], rr_w.at[a, side], at_y(1 if side == 0 else 3))

    def gather_partner(a, which):
        src = slab(lax.rem(y + (0, 3, 1, 2)[which], NY), a)
        return rcopy(src, src, ps_w.at[a, which], pr_w.at[a, which], partner)

    far_first = (4, 3, 5, 2, 6, 1, 7)
    for a in range(2):
        for d in far_first:
            gather_z(a, d).start()

    wall[z, y, k] = w_ref[...]
    kwin[pl.ds(2 * TOK, TOK)] = k_ref[...]
    vwin[pl.ds(2 * TOK, TOK)] = v_ref[...]
    dwin[2] = doc_ref[...]
    dk[...] = jnp.zeros_like(dk)
    dv[...] = jnp.zeros_like(dv)

    for i in range(3):
        halo_next(i).wait_recv()

        @pl.when(k == 0)
        def _():
            halo_relay(i).start()

    for i in range(3):
        halo_far(i).wait_recv()

    def gather_after_z(a):
        for d in range(1, NZ):
            gather_z(a, d).wait_recv()
        gather_y(a, 0).start()
        gather_y(a, 1).start()
        gather_partner(a, 0).start()

    def gather_after_y(a):
        for side in range(2):
            gather_y(a, side).wait_recv()
            gather_relay(a, side).start()
            gather_partner(a, 1 + side).start()

    def gather_after_relay(a):
        for side in range(2):
            gather_relay(a, side).wait_recv()
        gather_partner(a, 3).start()

    gather_after_z(0)

    doc_row = dwin[2].astype(F32)
    start = jnp.zeros((1, TOK), F32)
    for p in range(3):
        column = jnp.broadcast_to(dwin[p].astype(F32), (128, TOK)).T
        counts = [
            jnp.sum(jnp.where(column < doc_row[:, 128 * b : 128 * b + 128], 1.0, 0.0), axis=0, keepdims=True)
            for b in range(TOK // 128)
        ]
        count = jnp.concatenate(counts, 1)
        start = start + (jnp.where(c >= 2 - p, count, float(TOK)) if p < 2 else count)
    start = start.astype(I32)
    for b in range(2):
        st_ref[b] = start[:, QB * b : QB * b + QB] - QB * b

    k_turned = kwin[...].astype(F32).T.astype(BF)
    v_turned = vwin[...].astype(F32).T.astype(BF)
    for b in range(2):
        kt[b] = k_turned[:, QB * b : QB * b + KW]
        vt[b] = v_turned[:, QB * b : QB * b + KW]

    @pl.loop(0, 2 * HEADS)
    def _(t):
        b = lax.div(t, HEADS)
        h = lax.rem(t, HEADS)
        rows = pl.ds(al(b * QB, QB), QB)
        heads = pl.ds(al(h * HEAD, HEAD), HEAD)
        lanes = pl.ds(al(h * QB, QB), QB)
        scores = nt(kwin[pl.ds(al(b * QB, QB), KW), :], q_ref[rows, heads])
        key_at = lax.broadcasted_iota(I32, (KW, QB), 0)
        last = lax.broadcasted_iota(I32, (1, QB), 1) + 2 * TOK
        scores = jnp.where((key_at >= st_ref[b]) & (key_at <= last), scores, MASKED)
        top = jnp.max(scores, axis=0, keepdims=True)
        weights = jnp.exp2(scores * EXP_SCALE - top * EXP_SCALE)
        total = 1.0 / jnp.sum(weights, axis=0, keepdims=True)
        weights = weights.astype(BF)
        pbuf[b, :, lanes] = weights
        inv_l[t] = total
        turned = nn(vt[b], weights) * total
        att_t[heads, rows] = turned.astype(BF)
        att[rows, heads] = turned.T.astype(BF)

        @pl.when(t == 1)
        def _():
            gather_after_z(1)

        @pl.when(t == 3)
        def _():
            gather_after_y(0)

        @pl.when(t == 6)
        def _():
            gather_after_y(1)

    cot_copy.wait()

    @pl.loop(0, NZ)
    def _(zz):
        term = nn(att_t[...], cot[:, pl.ds(al(zz * TOK, TOK), TOK)]).astype(BF)
        for yy in range(NY):
            gbuf[zz, yy] = term[:, 128 * yy : 128 * yy + 128]

    def pair_send(q):
        return rcopy(
            gbuf.at[:, :, pl.ds(al((1 - k) * 256 + 128 * q, 128), 128), :],
            drecv.at[q], ds_s.at[q], dr_s.at[q], partner,
        )

    for q in range(2):
        pair_send(q).start()

    for a in range(2):
        gather_after_relay(a)
    for a in range(2):
        for which in range(4):
            gather_partner(a, which).wait_recv()

    def layer_term(r):
        owner = lax.rem(x + r, NX)

        @pl.loop(0, 2)
        def _(e):
            rows = wall[owner * 2 + e].reshape(TOK, TOK)
            lbuf[r, e] = nt(att[...], rows).astype(BF)

    def x_first(side):
        return rcopy(lbuf.at[2, side], xr1.at[side], x1s.at[side], x1r.at[side], at_x(1 if side == 0 else 3))

    def x_second(side, e):
        return rcopy(
            lbuf.at[1 if side == 0 else 3, e], xr2.at[side, e], x2s.at[side, e], x2r.at[side, e],
            at_x(1 if side == 0 else 3),
        )

    layer_term(2)
    x_first(0).start()
    x_first(1).start()
    layer_term(1)
    x_second(0, 1).start()
    layer_term(3)
    x_second(1, 0).start()
    layer_term(0)

    def y_first(q, side):
        return rcopy(
            gh.at[q, lax.rem(y + 2, NY), pl.ds(4 * side, 4)], yr1.at[q, side],
            y1s.at[q, side], y1r.at[q, side], at_y(1 if side == 0 else 3),
        )

    def y_second(q, side, e):
        return rcopy(
            gh.at[q, lax.rem(y + (1 if side == 0 else 3), NY), pl.ds(4 * e, 4)], yr2.at[q, side, e],
            y2s.at[q, side, e], y2r.at[q, side, e], at_y(1 if side == 0 else 3),
        )

    def grad_pair(q):
        pair_send(q).wait_recv()
        rows = pl.ds(al(k * 256 + 128 * q, 128), 128)

        @pl.loop(0, NZ)
        def _(zz):
            for yy in range(NY):
                gh[q, yy, zz] = (gbuf[zz, yy, rows, :].astype(F32) + drecv[q, zz, yy].astype(F32)).astype(BF)

        y_first(q, 0).start()
        y_first(q, 1).start()
        y_second(q, 0, 1).start()
        y_second(q, 1, 0).start()

    def grad_y_first(q):
        for side in range(2):
            y_first(q, side).wait_recv()
            owner = lax.rem(y + (1 if side == 0 else 3), NY)
            here = pl.ds(4 * side, 4)
            gh[q, owner, here] = (gh[q, owner, here].astype(F32) + yr1[q, side].astype(F32)).astype(BF)
            y_second(q, side, side).start()

    def grad_z(q, d):
        return rcopy(yh.at[q, lax.rem(z + d, NZ)], zr.at[q, d - 1], zs_g.at[q, d], zr_g.at[q, d], at_z(d))

    def grad_y_last(q):
        for side in range(2):
            for e in range(2):
                y_second(q, side, e).wait_recv()
        for e in range(2):
            here = pl.ds(4 * e, 4)
            total = gh[q, y, here].astype(F32) + yr2[q, 0, e].astype(F32) + yr2[q, 1, e].astype(F32)
            yh[q, here] = total.astype(BF)
        for d in far_first:
            grad_z(q, d).start()

    for q in range(2):
        grad_pair(q)

    @pl.loop(0, 2)
    def _(n):
        lanes = pl.ds(al(n * 256, 256), 256)
        d_o[:, lanes] = nn(cot[...], wall[:, :, :, :, lanes].reshape(4096, 256)).astype(BF)

    def x_add(side):
        x_first(side).wait_recv()
        r = 1 if side == 0 else 3
        lbuf[r, side] = (lbuf[r, side].astype(F32) + xr1[side].astype(F32)).astype(BF)
        x_second(side, side).start()

    @pl.loop(0, 2)
    def _(b):
        rows = pl.ds(al(b * QB, QB), QB)
        keys = pl.ds(al(b * QB, QB), KW)

        @pl.loop(0, HEADS)
        def _(h):
            heads = pl.ds(al(h * HEAD, HEAD), HEAD)
            lanes = pl.ds(al(h * QB, QB), QB)
            total = inv_l[b * HEADS + h]
            grad = d_o[rows, heads]
            turned = grad.astype(F32).T
            delta = jnp.sum(turned * att_t[heads, rows].astype(F32), axis=0, keepdims=True)
            dots = nt(vwin[keys, :], grad)
            shifted = (pbuf[b, :, lanes].astype(F32) * ((dots - delta) * (total * SCALE))).astype(BF)
            dsbuf[:, lanes] = shifted
            qg_ref[rows, heads] = nn(kt[b], shifted).T.astype(BF)
            dos[lanes, :] = (turned * total).T.astype(BF)
            qs[lanes, :] = q_ref[rows, heads]

            t = b * HEADS + h

            @pl.when(t == 1)
            def _():
                x_add(0)
                x_add(1)
                grad_y_first(0)

            @pl.when(t == 3)
            def _():
                grad_y_first(1)

            @pl.when(t == 5)
            def _():
                grad_y_last(0)

        dk[keys, :] += nn(dsbuf[...], qs[...])
        dv[keys, :] += nn(pbuf[b], dos[...])

    def grad_back(s):
        return rcopy(gks.at[s], gkr.at[s], gs.at[s], gr.at[s], at_ctx(s - 2))

    for s in range(2):
        gks[s, 0] = dk[pl.ds(s * TOK, TOK)].astype(BF)
        gks[s, 1] = dv[pl.ds(s * TOK, TOK)].astype(BF)
        grad_back(s).start()

    grad_y_last(1)

    sums = []
    for q in range(2):
        total = yh[q, z].astype(F32)
        for d in range(1, NZ):
            grad_z(q, d).wait_recv()
            total = total + zr[q, d - 1].astype(F32)
        sums.append(total.T)
    turned = jnp.concatenate(sums, 1).astype(BF)
    fts[0] = turned[0:64]
    fts[1] = turned[64:128]

    final = rcopy(fts.at[1 - k], frec, fs, fr, partner)
    final.start()

    for s in range(2):
        grad_back(s).wait_recv()
    for n, (acc, ref) in enumerate(((dk, kg_ref), (dv, vg_ref))):
        total = acc[pl.ds(2 * TOK, TOK)] + gkr[0, n].astype(F32) + gkr[1, n].astype(F32)
        ref[...] = total.astype(BF)

    final.wait_recv()
    mine, other = fts[k], frec[...]
    pg_ref[:, 0:256] = jnp.where(k == 0, mine, other)
    pg_ref[:, 256:512] = jnp.where(k == 0, other, mine)

    for e in range(2):
        for side in range(2):
            x_second(side, e).wait_recv()
        total = lbuf[0, e].astype(F32) + xr2[0, e].astype(F32) + xr2[1, e].astype(F32)
        out_ref[:, 512 * e : 512 * e + 512] = total.astype(BF)

    for i in range(3):
        halo_next(i).wait_send()

        @pl.when(k == 0)
        def _():
            halo_far(i).wait_send()
            halo_relay(i).wait_send()

    for a in range(2):
        for d in range(1, NZ):
            gather_z(a, d).wait_send()
        for side in range(2):
            gather_y(a, side).wait_send()
            gather_relay(a, side).wait_send()
        for which in range(4):
            gather_partner(a, which).wait_send()
    for q in range(2):
        pair_send(q).wait_send()
        for side in range(2):
            y_first(q, side).wait_send()
            for e in range(2):
                y_second(q, side, e).wait_send()
        for d in range(1, NZ):
            grad_z(q, d).wait_send()
    final.wait_send()
    for side in range(2):
        x_first(side).wait_send()
        for e in range(2):
            x_second(side, e).wait_send()
    for s in range(2):
        grad_back(s).wait_send()


def body(doc_ids, rotated_queries, rotated_keys, value_matrix, out_proj, cotangent):
    vmem = pl.BlockSpec(memory_space=pltpu.VMEM)
    shape = jax.ShapeDtypeStruct

    def buf(*dims, kind=BF):
        return pltpu.VMEM(dims, kind)

    return tuple(
        pl.pallas_call(
            kernel,
            out_shape=(
                shape((TOK, 1024), BF), shape((TOK, TOK), BF), shape((TOK, HEAD), BF),
                shape((TOK, HEAD), BF), shape((64, TOK), BF),
            ),
            in_specs=[vmem] * 5 + [pl.BlockSpec(memory_space=pl.ANY)],
            out_specs=(vmem,) * 5,
            scratch_shapes=[
                buf(TOK, 4096), buf(WIN, HEAD), buf(WIN, HEAD), buf(3, 1, TOK, kind=I32),
                buf(2, HEAD, KW), buf(2, HEAD, KW), buf(NZ, NY, 2, 64, TOK), buf(2, 1, QB, kind=I32),
                buf(2, KW, HEADS * QB), buf(KW, HEADS * QB), buf(TOK, TOK), buf(TOK, TOK),
                buf(2 * HEADS, 1, QB, kind=F32), buf(TOK, TOK), buf(HEADS * QB, HEAD), buf(HEADS * QB, HEAD),
                buf(WIN, HEAD, kind=F32), buf(WIN, HEAD, kind=F32),
                buf(NZ, NY, TOK, 128), buf(2, NZ, NY, 128, 128), buf(2, NY, NZ, 128, 128),
                buf(2, 2, 4, 128, 128), buf(2, 2, 2, 4, 128, 128), buf(2, NZ, 128, 128),
                buf(2, NZ - 1, 128, 128), buf(2, 64, 256), buf(64, 256),
                buf(NX, 2, TOK, TOK), buf(2, TOK, TOK), buf(2, 2, TOK, TOK),
                buf(2, 2, TOK, HEAD), buf(2, 2, TOK, HEAD),
                DMA, DMA((3, 3)), DMA((2, 3)), DMA((2, NZ)), DMA((2, NZ)), DMA((2, 2)), DMA((2, 2)),
                DMA((2, 2)), DMA((2, 2)), DMA((2, 4)), DMA((2, 4)),
                DMA((2,)), DMA((2,)), DMA((2, 2)), DMA((2, 2)), DMA((2, 2, 2)), DMA((2, 2, 2)),
                DMA((2, NZ)), DMA((2, NZ)), DMA, DMA, DMA((2,)), DMA((2,)), DMA((2, 2)), DMA((2, 2)),
                DMA((2,)), DMA((2,)),
            ],
            compiler_params=pltpu.CompilerParams(
                collective_id=0, has_side_effects=True, vmem_limit_bytes=64 * 1024 * 1024 - 65536
            ),
        )(doc_ids.reshape(1, TOK), rotated_queries, rotated_keys, value_matrix, out_proj, cotangent)
    )


def solution(mesh):
    in_specs = (P("ctx"), P("ctx", "hg"), P("ctx", "hg"), P("ctx", "hg"), P("ctx", "hg"), P("ctx", None))
    out_specs = (P("ctx", "hg"),) * 5
    return jax.shard_map(body, mesh=mesh, in_specs=in_specs, out_specs=out_specs, check_vma=False)
```

time: 324 us -> 102 us (0.31)
  waiting for transfers between devices: 212 us -> 0 us
  Pallas kernels: 0 us -> 92.8 us
  matrix products: 38.7 us -> 0 us
  starting transfers between devices: 27.3 us -> 0 us
  between operations: 14.4 us -> 0.64 us
  local copies, waits for them, and re-layouts: 20.9 us -> 8.74 us
  other arithmetic: 10.5 us -> 0 us
    unnamed x4 -> x0, waiting for transfers between devices: 104 us -> none
    pallas_call x0 -> x1, Pallas kernels: none -> 92.8 us  [body(): pl.pallas_call(kernel, out_shape=(shape((TOK, 1024), BF), shape((TOK, TOK...]
    reduce_scatter x1 -> x0, waiting for transfers between devices: 53.7 us -> none  [body(): lax.psum_scatter(partial_value.astype(jnp.bfloat16), 'hg', scatter_dimens...]
    all_gather x1 -> x0, waiting for transfers between devices: 47.7 us -> none  [body(): lax.all_gather(out_proj, 'ctx', axis=0, tiled=True)]
    dot_general x27 -> x0, matrix products: 38.7 us -> none  [the longest x9 16 us: contract_last(): lax.dot_general(left_side, right_side, (((1,), (1,)), ((), ())), preferre...]
    ppermute x10 -> x0, starting transfers between devices: 26.9 us -> none  [from_behind(): return lax.ppermute(value, axis, pairs)]
    unnamed x58 -> x5, local copies, waits for them, and re-layouts: 19 us -> 8.74 us
    ppermute x10 -> x0, waiting for transfers between devices: 6.02 us -> none  [from_behind(): return lax.ppermute(value, axis, pairs)]
  transfers between devices with their start and end apart: 13 -> 0, of which waited for: 6 -> 0; matrix products, arithmetic and copies ran while one was open for 13% -> 0% of each run, Pallas kernels for 0% -> 0%
where the time goes in v1:
time: 102 us
  Pallas kernels  92.8 us (91%)
  local copies, waits for them, and re-layouts  8.74 us (9%)
    pallas_call x1, Pallas kernels, body(): pl.pallas_call(kernel, out_shape=(shape((TOK, 1024), BF), shape((TOK, TOK...  92.8 us
    unnamed x5, local copies, waits for them, and re-layouts  8.74 us

profile of v1, /device:TPU:1, one launch (start us, length us, event | category | flops | bytes accessed | tf_op | source)
XLA Modules:
  0.0 102.2 jit_solution(2027867427627119369)
XLA Ops:
  0.6 92.8 %shard_map.101 = (bf16[512,1024]{1,0:T(8,128)(2,1)}, bf16[512,512]{1,0:T(8,128)(2,1)}, bf16[512,128]{1,0:T(8,128)(2,1)}, bf16[512,128]{1,0:T(8,128)(2,1)}, bf16[64,512]{1,0:T(8,128)(2,1)}) custom-call(s32[1,512]{1,0:T(1,128)} %bitcast.1, bf16[512,512]{1,0:T(8,128)(2,1)} %q_ref.1, bf16[512,128]{1,0:T(8,128)(2,1)} %k_ref.1, bf16[512,128]{1,0:T(8,128)(2,1)} %v_ref.1, ...), custom_call_target="tpu_custom_call" | custom-call | tf_op jit(solution)/shard_map/pallas_call | solution.py:456
  93.4 2.3 %copy.16 = bf16[512,1024]{1,0:T(8,128)(2,1)} copy(bf16[512,1024]{1,0:T(8,128)(2,1)} %get-tuple-element.10) | data formatting | bytes 2097152
  95.7 1.9 %copy.17 = bf16[512,512]{1,0:T(8,128)(2,1)} copy(bf16[512,512]{1,0:T(8,128)(2,1)} %get-tuple-element.11) | data formatting | bytes 1048576
  97.6 1.6 %copy.18 = bf16[512,128]{1,0:T(8,128)(2,1)} copy(bf16[512,128]{1,0:T(8,128)(2,1)} %get-tuple-element.12) | data formatting | bytes 262144
  99.1 1.6 %copy.19 = bf16[512,128]{1,0:T(8,128)(2,1)} copy(bf16[512,128]{1,0:T(8,128)(2,1)} %get-tuple-element.13) | data formatting | bytes 262144
  100.7 1.5 %copy.20 = bf16[64,512]{1,0:T(8,128)(2,1)} copy(bf16[64,512]{1,0:T(8,128)(2,1)} %get-tuple-element.14) | data formatting | bytes 131072

commit v2 on v1

v2 whole, which is shorter than its diff:
```python
import jax
import jax.numpy as jnp
from jax import lax
from jax.experimental import pallas as pl
from jax.experimental.pallas import tpu as pltpu
from jax.sharding import PartitionSpec as P

MESH = pl.DeviceIdType.MESH
BF = jnp.bfloat16
F32 = jnp.float32
I32 = jnp.int32
DMA = pltpu.SemaphoreType.DMA

HEAD = 128
HEADS = 4
TOK = 512
QB = 256
KW = 1280
WIN = 1536
NX, NY, NZ = 4, 4, 8
CTX = 64
SCALE = HEAD ** (-0.5)
EXP_SCALE = SCALE * 1.4426950408889634
MASKED = -1e30
VMEM_LIMIT = 64 * 1024 * 1024 - 65536
UNITS = (
    (0, (0, 0)), (1, (0, 0)), (0, (3, 1)), (1, (3, 1)), (0, (1, 3)), (1, (1, 3)), (0, (2, 2)), (1, (2, 2)),
)
CHUNKS = ((0, 112), (112, 112), (224, 32))


def nn(a, b):
    return jnp.dot(a, b, preferred_element_type=F32)


def nt(a, b):
    return lax.dot_general(a, b, (((1,), (1,)), ((), ())), preferred_element_type=F32)


def al(value, by):
    return pl.multiple_of(value, by)


def kernel(
    doc_hbm, q_hbm, k_hbm, v_hbm, w_hbm, cot_hbm,
    out_hbm, qg_hbm, kg_hbm, vg_hbm, pg_hbm,
    doc_ref, q_ref, k_ref, v_ref, w_ref, out_ref, qg_ref, kg_ref, vg_ref, pg_ref,
    cot, kwin, vwin, dwin, kt, vt, wall, st_ref, pbuf, dsbuf, att_t, att, inv_l, delta, d_o, dos, qs, dk, dv,
    gbuf, drecv, gh, yr1, yr2, yh, zr, gz, zre, gy, yrl, fts, frec, lbuf, xr1, xr2, gks, gkr,
    vrel, vs, vr, cot_sem, in_sem, out_sem, hs, hr, az_s, az_r, ao_s, ao_r, ys_w, yr_w, rs_w, rr_w, ps_w, pr_w,
    ds_s, dr_s, y1s, y1r, y2s, y2r, zs_g, zr_g, zs_e, zr_e, ys_l, yr_l, fs, fr, x1s, x1r, x2s, x2r, gs, gr,
):
    c = lax.axis_index("ctx")
    x = lax.axis_index("hg")
    z = lax.div(c, 8)
    y = lax.rem(lax.div(c, 2), NY)
    k = lax.rem(c, 2)

    def at_ctx(by):
        return (lax.rem(c + by + CTX, CTX), x)

    def at_z(by):
        return (lax.rem(z + by, NZ) * 8 + y * 2 + k, x)

    def at_y(by):
        return (z * 8 + lax.rem(y + by, NY) * 2 + k, x)

    def at_x(by):
        return (c, lax.rem(x + by, NX))

    partner = (z * 8 + y * 2 + (1 - k), x)

    def rcopy(src, dst, send, recv, device):
        return pltpu.make_async_remote_copy(
            src_ref=src, dst_ref=dst, send_sem=send, recv_sem=recv,
            device_id=device, device_id_type=MESH,
        )

    barrier = pltpu.get_barrier_semaphore()
    peers = [partner, at_y(1), at_y(3), at_x(1), at_x(3), at_ctx(1), at_ctx(2), at_ctx(-1), at_ctx(-2)]
    peers += [at_z(d) for d in range(1, NZ)]
    for peer in peers:
        pl.semaphore_signal(barrier, inc=1, device_id=peer, device_id_type=MESH)
    ins = ((w_hbm, w_ref), (k_hbm, k_ref), (doc_hbm, doc_ref), (v_hbm, v_ref), (q_hbm, q_ref))
    ins = [pltpu.make_async_copy(src, dst, in_sem.at[i]) for i, (src, dst) in enumerate(ins)]
    outs = ((out_ref, out_hbm), (qg_ref, qg_hbm), (kg_ref, kg_hbm), (vg_ref, vg_hbm), (pg_ref, pg_hbm))
    outs = [pltpu.make_async_copy(src, dst, out_sem.at[i]) for i, (src, dst) in enumerate(outs)]
    cot_copy = pltpu.make_async_copy(cot_hbm, cot, cot_sem)
    for copy in ins:
        copy.start()
    cot_copy.start()
    for copy in ins:
        copy.wait()
    pl.semaphore_wait(barrier, len(peers))

    own_parts = ((doc_ref, dwin, 0), (k_ref, kwin, 1), (v_ref, vwin, 2))

    def piece(ref, index, at):
        return ref.at[at] if index == 0 else ref.at[pl.ds(at * TOK, TOK)]

    def halo_next(i):
        mine, ref, n = own_parts[i]
        return rcopy(mine, piece(ref, n, 1), hs.at[0, n], hr.at[1, n], at_ctx(1))

    def halo_far(i):
        mine, ref, n = own_parts[i]
        return rcopy(mine, piece(ref, n, 0), hs.at[1, n], hr.at[0, n], at_ctx(2))

    def halo_relay(i):
        _, ref, n = own_parts[i]
        return rcopy(piece(ref, n, 1), piece(ref, n, 0), hs.at[2, n], hr.at[0, n], partner)

    def shard(zz):
        return wall.at[zz, y, k]

    def gather_z(way, d):
        to = at_z(d if way == 0 else NZ - d)
        return rcopy(w_ref, shard(z), az_s.at[way, d - 1], az_r.at[way, d - 1], to)

    def gather_on(way, d):
        zz = lax.rem(z + (NZ - 2 if way == 0 else 2), NZ)
        rows = pl.ds(0, 64) if d == 1 else pl.ds(32 * way, 32)
        src = wall.at[zz, y, k, rows]
        return rcopy(src, src, ao_s.at[way, d - 1], ao_r.at[way, d - 1], at_z(d if way == 0 else NZ - d))

    def slab(back, part):
        return wall.at[pl.ds(4 * part, 4), lax.rem(y + back, NY), k]

    def gather_y(side, part):
        return rcopy(slab(0, part), slab(0, part), ys_w.at[side, part], yr_w.at[side, part], at_y(1 if side == 0 else 3))

    def gather_relay(side):
        src = slab(3 if side == 0 else 1, side)
        return rcopy(src, src, rs_w.at[side], rr_w.at[side], at_y(1 if side == 0 else 3))

    def pass_on(back, part):
        return rcopy(slab(back, part), slab(back, part), ps_w.at[back, part], pr_w.at[back, part], partner)

    def gather_first_parts():
        for side in range(2):
            gather_y(side, side).wait_recv()
            gather_relay(side).start()
            pass_on(3 if side == 0 else 1, side).start()

    def gather_second_parts():
        for side in range(2):
            gather_y(side, 1 - side).wait_recv()
            pass_on(3 if side == 0 else 1, 1 - side).start()

    def gather_far_parts():
        for side in range(2):
            gather_relay(side).wait_recv()
            pass_on(2, side).start()

    def slabs_ready(backs):
        for part in range(2):
            pass_on(backs[part], part).wait_recv()

    def halo_starts(i):
        halo_next(i).start()

        @pl.when(k == 0)
        def _():
            halo_far(i).start()

    last_y = y == NY - 1
    first_y = y == 0
    values_up = rcopy(v_ref, vrel, vs.at[0], vr, at_y(1))
    values_on = rcopy(vrel, piece(vwin, 2, 0), vs.at[1], hr.at[0, 2], at_z(1))
    values_swap = rcopy(piece(vwin, 2, 0), piece(vwin, 2, 1), hs.at[2, 2], hr.at[1, 2], partner)

    halo_starts(0)
    halo_starts(1)

    @pl.when(jnp.logical_not(last_y))
    def _():
        halo_starts(2)

    @pl.when(last_y)
    def _():
        values_up.start()

        @pl.when(k == 0)
        def _():
            halo_next(2).start()

    for d in (2, 1):
        for way in range(2):
            gather_z(way, d).start()

    wall[z, y, k] = w_ref[...]
    kwin[pl.ds(2 * TOK, TOK)] = k_ref[...]
    vwin[pl.ds(2 * TOK, TOK)] = v_ref[...]
    dwin[2] = doc_ref[...]
    dk[...] = jnp.zeros_like(dk)
    dv[...] = jnp.zeros_like(dv)

    def gather_middle():
        for way in range(2):
            gather_z(way, 2).wait_recv()
            gather_on(way, 2).start()
            gather_on(way, 1).start()

    def halo_arrives(i):
        halo_next(i).wait_recv()

        @pl.when(k == 0)
        def _():
            halo_relay(i).start()

    def gather_along_y():
        for way in range(2):
            gather_z(way, 1).wait_recv()
            gather_on(way, 1).wait_recv()
        for way in range(2):
            gather_on(way, 2).wait_recv()
        for part in range(2):
            for side in range(2):
                gather_y(side, part if side == 0 else 1 - part).start()
        for part in range(2):
            pass_on(0, part).start()

    halo_arrives(0)
    halo_arrives(1)

    @pl.when(jnp.logical_not(last_y))
    def _():
        gather_middle()

    for i in range(2):
        halo_far(i).wait_recv()

    doc_row = dwin[2].astype(F32)
    start = jnp.zeros((1, TOK), F32)
    for p in range(3):
        column = jnp.broadcast_to(dwin[p].astype(F32), (128, TOK)).T
        counts = [
            jnp.sum(jnp.where(column < doc_row[:, 128 * b : 128 * b + 128], 1.0, 0.0), axis=0, keepdims=True)
            for b in range(TOK // 128)
        ]
        count = jnp.concatenate(counts, 1)
        start = start + (jnp.where(c >= 2 - p, count, float(TOK)) if p < 2 else count)
    start = start.astype(I32)
    for b in range(2):
        st_ref[b] = start[:, QB * b : QB * b + QB] - QB * b

    def x_first(u, side):
        return rcopy(lbuf.at[u, 2, side], xr1.at[u, side], x1s.at[u, side], x1r.at[u, side], at_x(1 if side == 0 else 3))

    def x_second(u, side, e):
        return rcopy(
            lbuf.at[u, 1 if side == 0 else 3, e], xr2.at[u, side, e], x2s.at[u, side, e], x2r.at[u, side, e],
            at_x(1 if side == 0 else 3),
        )

    def layer_unit(u):
        b, backs = UNITS[u]
        for part in range(2):
            rows = wall[pl.ds(4 * part, 4), lax.rem(y + backs[part], NY)].reshape(TOK, TOK)
            term = nt(att[pl.ds(b * QB, QB)], rows).astype(BF)
            for owner in range(2):
                for e in range(2):
                    at = 256 * owner + 128 * e
                    lbuf[u, lax.rem(2 * part + owner - x + NX, NX), e] = term[:, at : at + 128]
        x_first(u, 0).start()
        x_first(u, 1).start()
        x_second(u, 0, 1).start()
        x_second(u, 1, 0).start()

    def layer_second(u):
        for side in range(2):
            x_first(u, side).wait_recv()
            r = 1 if side == 0 else 3
            lbuf[u, r, side] = (lbuf[u, r, side].astype(F32) + xr1[u, side].astype(F32)).astype(BF)
            x_second(u, side, side).start()

    def layer_last(u):
        b, backs = UNITS[u]
        back = jnp.where(x < 2, backs[0], backs[1])
        for e in range(2):
            for side in range(2):
                x_second(u, side, e).wait_recv()
            total = lbuf[u, 0, e].astype(F32) + xr2[u, 0, e].astype(F32) + xr2[u, 1, e].astype(F32)
            lanes = pl.ds(al(512 * e + 128 * lax.rem(y + back, NY), 128), 128)
            out_ref[pl.ds(b * QB, QB), lanes] = total.astype(BF)

    def layer_sent(u):
        for side in range(2):
            x_first(u, side).wait_send()
            for e in range(2):
                x_second(u, side, e).wait_send()

    def attend(t):
        b = lax.div(t, HEADS)
        h = lax.rem(t, HEADS)
        rows = pl.ds(al(b * QB, QB), QB)
        heads = pl.ds(al(h * HEAD, HEAD), HEAD)
        scores = nt(kwin[pl.ds(al(b * QB, QB), KW), :], q_ref[rows, heads])
        key_at = lax.broadcasted_iota(I32, (KW, QB), 0)
        last = lax.broadcasted_iota(I32, (1, QB), 1) + 2 * TOK
        scores = jnp.where((key_at >= st_ref[b]) & (key_at <= last), scores, MASKED)
        top = jnp.max(scores, axis=0, keepdims=True)
        weights = jnp.exp2(scores * EXP_SCALE - top * EXP_SCALE)
        inv_l[t] = 1.0 / jnp.sum(weights, axis=0, keepdims=True)
        pbuf[b, :, pl.ds(al(h * QB, QB), QB)] = weights.astype(BF)

    def gather_values(t):
        b = lax.div(t, HEADS)
        h = lax.rem(t, HEADS)
        rows = pl.ds(al(b * QB, QB), QB)
        heads = pl.ds(al(h * HEAD, HEAD), HEAD)
        turned = nn(vt[b], pbuf[b, :, pl.ds(al(h * QB, QB), QB)]) * inv_l[t]
        att_t[heads, rows] = turned.astype(BF)
        att[rows, heads] = turned.T.astype(BF)

    @pl.loop(0, HEADS)
    def _(t):
        attend(t)

        @pl.when((t == 0) & first_y)
        def _():
            values_up.wait_recv()
            values_on.start()

        @pl.when((t == 1) & last_y)
        def _():
            gather_middle()

        @pl.when((t == 1) & jnp.logical_not(last_y))
        def _():
            gather_along_y()

    @pl.when(first_y)
    def _():
        halo_far(2).wait_recv()

        @pl.when(k == 1)
        def _():
            values_swap.start()

        halo_next(2).wait_recv()

    @pl.when(jnp.logical_not(first_y))
    def _():
        halo_arrives(2)
        halo_far(2).wait_recv()

    v_turned = vwin[...].astype(F32).T.astype(BF)
    for b in range(2):
        vt[b] = v_turned[:, QB * b : QB * b + KW]

    odd = lax.rem(y, 2) == 1
    even = jnp.logical_not(odd)

    @pl.loop(0, HEADS)
    def _(t):
        gather_values(t)

        @pl.when((t == 0) & last_y)
        def _():
            gather_along_y()

    slabs_ready((0, 0))
    layer_unit(0)

    @pl.loop(HEADS, 2 * HEADS)
    def _(t):
        attend(t)
        gather_values(t)

        @pl.when((t == 6) & odd)
        def _():
            gather_first_parts()

    layer_unit(1)

    def pair_send(quarter):
        zs = pl.ds(al(2 * quarter, 2), 2)
        return rcopy(
            gbuf.at[zs, :, pl.ds(al((1 - k) * 256, 256), 256), :], drecv.at[zs],
            ds_s.at[quarter], dr_s.at[quarter], partner,
        )

    cot_copy.wait()

    @pl.loop(0, NZ)
    def _(zz):
        term = nn(att_t[...], cot[:, pl.ds(al(zz * TOK, TOK), TOK)]).astype(BF)
        for yy in range(NY):
            gbuf[zz, yy] = term[:, 128 * yy : 128 * yy + 128]

        @pl.when(lax.rem(zz, 2) == 1)
        def _():
            pair_send(lax.div(zz, 2)).start()

        @pl.when(((zz == 0) & odd) | ((zz == 5) & even))
        def _():
            slabs_ready((3, 1))
            layer_unit(2)
            layer_unit(3)

        @pl.when((zz == 2) & even)
        def _():
            gather_first_parts()

        @pl.when((zz == 4) & odd)
        def _():
            gather_second_parts()

    layer_second(0)

    def y_first(q, side):
        return rcopy(
            gh.at[q, lax.rem(y + 2, NY), pl.ds(4 * side, 4)], yr1.at[q, side],
            y1s.at[q, side], y1r.at[q, side], at_y(1 if side == 0 else 3),
        )

    def y_second(q, side, e):
        return rcopy(
            gh.at[q, lax.rem(y + (1 if side == 0 else 3), NY), pl.ds(4 * e, 4)], yr2.at[q, side, e],
            y2s.at[q, side, e], y2r.at[q, side, e], at_y(1 if side == 0 else 3),
        )

    def early_z(d):
        return rcopy(gz.at[lax.rem(z + d, NZ)], zre.at[d - 1], zs_e.at[d], zr_e.at[d], at_z(d))

    def late_y(d):
        return rcopy(gy.at[lax.rem(y + d, NY)], yrl.at[d - 1], ys_l.at[d], yr_l.at[d], at_y(d))

    far_first = (4, 3, 5, 2, 6, 1, 7)

    def grad_pair(q):
        low, rows = CHUNKS[q]
        mine, here = pl.ds(al(k * 256 + low, 16), rows), pl.ds(low, rows)

        @pl.loop(0, NZ)
        def _(zz):
            for yy in range(NY):
                total = (gbuf[zz, yy, mine, :].astype(F32) + drecv[zz, yy, here, :].astype(F32)).astype(BF)
                if q < 2:
                    gh[q, yy, zz] = total
                else:
                    gz[zz, yy] = total

        if q < 2:
            y_first(q, 0).start()
            y_first(q, 1).start()
            y_second(q, 0, 1).start()
            y_second(q, 1, 0).start()
        else:
            for d in far_first:
                early_z(d).start()

    def grad_y_first(q):
        for side in range(2):
            y_first(q, side).wait_recv()
            owner = lax.rem(y + (1 if side == 0 else 3), NY)
            here = pl.ds(4 * side, 4)
            gh[q, owner, here] = (gh[q, owner, here].astype(F32) + yr1[q, side].astype(F32)).astype(BF)
            y_second(q, side, side).start()

    def grad_z(q, d):
        return rcopy(yh.at[q, lax.rem(z + d, NZ)], zr.at[q, d - 1], zs_g.at[q, d], zr_g.at[q, d], at_z(d))

    def grad_y_last(q):
        for side in range(2):
            for e in range(2):
                y_second(q, side, e).wait_recv()
        for e in range(2):
            here = pl.ds(4 * e, 4)
            total = gh[q, y, here].astype(F32) + yr2[q, 0, e].astype(F32) + yr2[q, 1, e].astype(F32)
            yh[q, here] = total.astype(BF)
        for d in far_first:
            grad_z(q, d).start()

    def grad_early_z():
        total = gz[z].astype(F32)
        for d in range(1, NZ):
            early_z(d).wait_recv()
            total = total + zre[d - 1].astype(F32)
        gy[...] = total.astype(BF)
        for d in (2, 1, 3):
            late_y(d).start()

    for quarter in range(4):
        pair_send(quarter).wait_recv()
    for q in range(3):
        grad_pair(q)

    @pl.when(even)
    def _():
        gather_second_parts()

    slabs_ready((1, 3))
    layer_unit(4)
    layer_unit(5)
    layer_second(1)
    gather_far_parts()
    slabs_ready((2, 2))
    layer_unit(6)
    layer_unit(7)

    @pl.loop(0, 2)
    def _(n):
        lanes = pl.ds(al(n * 256, 256), 256)
        d_o[:, lanes] = nn(cot[...], wall[:, :, :, :, lanes].reshape(4096, 256)).astype(BF)

    grad_y_first(0)

    def prepare(b, h):
        rows = pl.ds(QB * b, QB)
        heads = pl.ds(al(h * HEAD, HEAD), HEAD)
        lanes = pl.ds(al(h * QB, QB), QB)
        turned = d_o[rows, heads].astype(F32).T
        delta[b * HEADS + h] = jnp.sum(turned * att_t[heads, rows].astype(F32), axis=0, keepdims=True)
        dos[b, lanes, :] = (turned * inv_l[b * HEADS + h]).T.astype(BF)
        qs[b, lanes, :] = q_ref[rows, heads]

    def shift(b, h, low, count):
        lanes = pl.ds(al(h * QB, QB), QB)
        here = pl.ds(low - QB * b, count)
        t = b * HEADS + h
        dots = nt(vwin[pl.ds(low, count), :], d_o[pl.ds(QB * b, QB), pl.ds(al(h * HEAD, HEAD), HEAD)])
        factor = (dots - delta[t]) * (inv_l[t] * SCALE)
        dsbuf[b, here, lanes] = (pbuf[b, here, lanes].astype(F32) * factor).astype(BF)

    def key_terms(b, low, count):
        keys, here = pl.ds(low, count), pl.ds(low - QB * b, count)
        dk[keys, :] += nn(dsbuf[b, here, :], qs[b])
        dv[keys, :] += nn(pbuf[b, here, :], dos[b])

    def shift_all(b, low, count, events):
        @pl.loop(0, HEADS)
        def _(h):
            if low < 2 * TOK:
                prepare(b, h)
            shift(b, h, low, count)
            for at, event in events:

                @pl.when(h == at)
                def _():
                    event()

        key_terms(b, low, count)

    shift_all(0, 0, 1024, ((0, lambda: layer_second(2)), (1, lambda: grad_y_first(1)), (2, lambda: layer_second(3))))
    grad_y_last(0)
    shift_all(1, QB, 768, ((0, lambda: layer_second(4)), (2, lambda: layer_second(5))))

    pair_back = rcopy(gks.at[1], gkr.at[1], gs.at[1], gr.at[1], partner)
    far_back = rcopy(gks.at[0], gkr.at[0], gs.at[0], gr.at[0], at_ctx(-2))
    for s in (1, 0):
        gks[s, 0] = dk[pl.ds(s * TOK, TOK)].astype(BF)
        gks[s, 1] = dv[pl.ds(s * TOK, TOK)].astype(BF)
        if s == 1:
            pair_back.start()

    @pl.when(k == 0)
    def _():
        far_back.start()

    grad_y_last(1)
    grad_early_z()
    layer_second(6)
    shift_all(0, 1024, QB, ())
    pair_back.wait_recv()

    @pl.when(k == 1)
    def _():
        for n, acc in enumerate((dk, dv)):
            gks[0, n] = (acc[pl.ds(0, TOK)] + gkr[1, n].astype(F32)).astype(BF)
        far_back.start()

    layer_second(7)
    shift_all(1, 1024, 2 * QB, ())
    k_turned = kwin[...].astype(F32).T.astype(BF)
    for b in range(2):
        kt[b] = k_turned[:, QB * b : QB * b + KW]

    @pl.loop(0, 2 * HEADS)
    def _(t):
        b = lax.div(t, HEADS)
        h = lax.rem(t, HEADS)
        grad = nn(kt[b], dsbuf[b, :, pl.ds(al(h * QB, QB), QB)])
        qg_ref[pl.ds(al(b * QB, QB), QB), pl.ds(al(h * HEAD, HEAD), HEAD)] = grad.T.astype(BF)

    outs[1].start()

    for u in range(6):
        layer_last(u)

    sums = []
    for q in range(2):
        total = yh[q, z].astype(F32)
        for d in range(1, NZ):
            grad_z(q, d).wait_recv()
            total = total + zr[q, d - 1].astype(F32)
        sums.append(total)
    total = gy[y].astype(F32)
    for d in range(1, NY):
        late_y(d).wait_recv()
        total = total + yrl[d - 1].astype(F32)
    sums.append(total)
    turned = jnp.concatenate(sums, 0).T.astype(BF)
    fts[0] = turned[0:64]
    fts[1] = turned[64:128]

    final = rcopy(fts.at[1 - k], frec, fs, fr, partner)
    final.start()

    for u in range(6, len(UNITS)):
        layer_last(u)
    outs[0].start()

    far_back.wait_recv()
    for n, (acc, ref) in enumerate(((dk, kg_ref), (dv, vg_ref))):
        near = jnp.where(k == 0, gkr[1, n].astype(F32), 0.0)
        ref[...] = (acc[pl.ds(2 * TOK, TOK)] + gkr[0, n].astype(F32) + near).astype(BF)
        outs[2 + n].start()

    final.wait_recv()
    mine, other = fts[k], frec[...]
    pg_ref[:, 0:256] = jnp.where(k == 0, mine, other)
    pg_ref[:, 256:512] = jnp.where(k == 0, other, mine)
    outs[4].start()

    for i in range(2):
        halo_next(i).wait_send()

        @pl.when(k == 0)
        def _():
            halo_far(i).wait_send()
            halo_relay(i).wait_send()

    @pl.when(jnp.logical_not(last_y))
    def _():
        halo_next(2).wait_send()

        @pl.when(k == 0)
        def _():
            halo_far(2).wait_send()

    @pl.when(last_y)
    def _():
        values_up.wait_send()

        @pl.when(k == 0)
        def _():
            halo_next(2).wait_send()

    @pl.when(jnp.logical_not(first_y) & (k == 0))
    def _():
        halo_relay(2).wait_send()

    @pl.when(first_y)
    def _():
        values_on.wait_send()

        @pl.when(k == 1)
        def _():
            values_swap.wait_send()

    for way in range(2):
        for d in (1, 2):
            gather_z(way, d).wait_send()
            gather_on(way, d).wait_send()
        gather_relay(way).wait_send()
        for part in range(2):
            gather_y(way, part).wait_send()
    for back in range(NY):
        for part in range(2):
            pass_on(back, part).wait_send()
    for quarter in range(4):
        pair_send(quarter).wait_send()
    for q in range(2):
        for side in range(2):
            y_first(q, side).wait_send()
            for e in range(2):
                y_second(q, side, e).wait_send()
        for d in range(1, NZ):
            grad_z(q, d).wait_send()
    for d in range(1, NZ):
        early_z(d).wait_send()
    for d in range(1, NY):
        late_y(d).wait_send()
    final.wait_send()
    for u in range(len(UNITS)):
        layer_sent(u)
    pair_back.wait_send()
    far_back.wait_send()

    for copy in outs:
        copy.wait()


def finish(*refs):
    sources, targets, held, read, wrote = refs[:5], refs[5:10], refs[10:15], refs[15], refs[16]
    reads = [pltpu.make_async_copy(sources[i], held[i], read.at[i]) for i in range(5)]
    writes = [pltpu.make_async_copy(held[i], targets[i], wrote.at[i]) for i in range(5)]
    for copy in reads:
        copy.start()
    for i in range(5):
        reads[i].wait()
        writes[i].start()
    for copy in writes:
        copy.wait()


def body(doc_ids, rotated_queries, rotated_keys, value_matrix, out_proj, cotangent):
    hbm = pl.BlockSpec(memory_space=pl.ANY)
    shape = jax.ShapeDtypeStruct

    def buf(*dims, kind=BF):
        return pltpu.VMEM(dims, kind)

    out_shape = (
        shape((TOK, 1024), BF), shape((TOK, TOK), BF), shape((TOK, HEAD), BF),
        shape((TOK, HEAD), BF), shape((64, TOK), BF),
    )
    results = tuple(
        pl.pallas_call(
            kernel,
            out_shape=out_shape,
            in_specs=[hbm] * 6,
            out_specs=(hbm,) * 5,
            scratch_shapes=[
                buf(1, TOK, kind=I32), buf(TOK, TOK), buf(TOK, HEAD), buf(TOK, HEAD), buf(64, TOK),
                buf(TOK, 1024), buf(TOK, TOK), buf(TOK, HEAD), buf(TOK, HEAD), buf(64, TOK),
                buf(TOK, 4096), buf(WIN, HEAD), buf(WIN, HEAD), buf(3, 1, TOK, kind=I32),
                buf(2, HEAD, KW), buf(2, HEAD, KW), buf(NZ, NY, 2, 64, TOK), buf(2, 1, QB, kind=I32),
                buf(2, KW, HEADS * QB), buf(2, KW, HEADS * QB), buf(TOK, TOK), buf(TOK, TOK),
                buf(2 * HEADS, 1, QB, kind=F32), buf(2 * HEADS, 1, QB, kind=F32), buf(TOK, TOK),
                buf(2, HEADS * QB, HEAD), buf(2, HEADS * QB, HEAD),
                buf(WIN, HEAD, kind=F32), buf(WIN, HEAD, kind=F32),
                buf(NZ, NY, TOK, 128), buf(NZ, NY, 256, 128), buf(2, NY, NZ, 112, 128),
                buf(2, 2, 4, 112, 128), buf(2, 2, 2, 4, 112, 128), buf(2, NZ, 112, 128), buf(2, NZ - 1, 112, 128),
                buf(NZ, NY, 32, 128), buf(NZ - 1, NY, 32, 128), buf(NY, 32, 128), buf(NY - 1, 32, 128),
                buf(2, 64, 256), buf(64, 256),
                buf(8, NX, 2, QB, 128), buf(8, 2, QB, 128), buf(8, 2, 2, QB, 128),
                buf(2, 2, TOK, HEAD), buf(2, 2, TOK, HEAD),
                buf(TOK, HEAD), DMA((2,)), DMA, DMA, DMA((5,)), DMA((5,)), DMA((3, 3)), DMA((2, 3)), DMA((2, 2)), DMA((2, 2)), DMA((2, 2)), DMA((2, 2)),
                DMA((2, 2)), DMA((2, 2)), DMA((2,)), DMA((2,)), DMA((NY, 2)), DMA((NY, 2)),
                DMA((4,)), DMA((4,)), DMA((2, 2)), DMA((2, 2)), DMA((2, 2, 2)), DMA((2, 2, 2)),
                DMA((2, NZ)), DMA((2, NZ)), DMA((NZ,)), DMA((NZ,)), DMA((NY,)), DMA((NY,)), DMA, DMA,
                DMA((8, 2)), DMA((8, 2)), DMA((8, 2, 2)), DMA((8, 2, 2)), DMA((2,)), DMA((2,)),
            ],
            compiler_params=pltpu.CompilerParams(
                collective_id=0, has_side_effects=True, vmem_limit_bytes=VMEM_LIMIT
            ),
        )(doc_ids.reshape(1, TOK), rotated_queries, rotated_keys, value_matrix, out_proj, cotangent)
    )
    return tuple(
        pl.pallas_call(
            finish,
            out_shape=out_shape,
            in_specs=[hbm] * 5,
            out_specs=(hbm,) * 5,
            scratch_shapes=[pltpu.VMEM(o.shape, o.dtype) for o in out_shape] + [DMA((5,)), DMA((5,))],
            compiler_params=pltpu.CompilerParams(vmem_limit_bytes=VMEM_LIMIT),
        )(*results)
    )


def solution(mesh):
    in_specs = (P("ctx"), P("ctx", "hg"), P("ctx", "hg"), P("ctx", "hg"), P("ctx", "hg"), P("ctx", None))
    out_specs = (P("ctx", "hg"),) * 5
    return jax.shard_map(body, mesh=mesh, in_specs=in_specs, out_specs=out_specs, check_vma=False)
```

time: 102 us -> 77.5 us (0.76)
  Pallas kernels: 92.8 us -> 76.6 us
  local copies, waits for them, and re-layouts: 8.74 us -> 0 us
    pallas_call x1 -> x2, Pallas kernels: 92.8 us -> 76.6 us  [the longest x1 74.1 us: body(): pl.pallas_call(kernel, out_shape=out_shape, in_specs=[hbm] * 6, out_specs...]
    unnamed x5 -> x0, local copies, waits for them, and re-layouts: 8.74 us -> none
where the time goes in v2:
time: 77.5 us; the launch traced here: 77.4 us
  Pallas kernels  76.6 us (99%)
  between operations  0.8 us (1%)
    pallas_call x1, Pallas kernels, body(): pl.pallas_call(kernel, out_shape=out_shape, in_specs=[hbm] * 6, out_specs...  74.1 us
    pallas_call x1, Pallas kernels, body(): pl.pallas_call(finish, out_shape=out_shape, in_specs=[hbm] * 5, out_specs...  2.55 us

profile of v2, /device:TPU:1, one launch (start us, length us, event | category | flops | bytes accessed | tf_op | source)
XLA Modules:
  0.0 77.4 jit_solution(17872194188618968230)
XLA Ops:
  0.6 74.1 %shard_map.101 = (bf16[512,1024]{1,0:T(8,128)(2,1)}, bf16[512,512]{1,0:T(8,128)(2,1)}, bf16[512,128]{1,0:T(8,128)(2,1)}, bf16[512,128]{1,0:T(8,128)(2,1)}, bf16[64,512]{1,0:T(8,128)(2,1)}) custom-call(s32[1,512]{1,0:T(1,128)} %bitcast.1, bf16[512,512]{1,0:T(8,128)(2,1)} %q_hbm.1, bf16[512,128]{1,0:T(8,128)(2,1)} %k_hbm.1, bf16[512,128]{1,0:T(8,128)(2,1)} %v_hbm.1, ...), custom_call_target="tpu_custom_call" | custom-call | tf_op jit(solution)/shard_map/pallas_call | solution.py:721
  74.7 2.5 %shard_map.102 = (bf16[512,1024]{1,0:T(8,128)(2,1)}, bf16[512,512]{1,0:T(8,128)(2,1)}, bf16[512,128]{1,0:T(8,128)(2,1)}, bf16[512,128]{1,0:T(8,128)(2,1)}, bf16[64,512]{1,0:T(8,128)(2,1)}) custom-call(bf16[512,1024]{1,0:T(8,128)(2,1)} %get-tuple-element.10.refs_0_, bf16[512,512]{1,0:T(8,128)(2,1)} %get-tuple-element.11.refs_1_, ...), custom_call_target="tpu_custom_call" | custom-call | tf_op jit(solution)/shard_map/pallas_call | solution.py:753

commit v3 on v2

--- a/solution.py
+++ b/solution.py
@@ -26,7 +26,7 @@
 UNITS = (
     (0, (0, 0)), (1, (0, 0)), (0, (3, 1)), (1, (3, 1)), (0, (1, 3)), (1, (1, 3)), (0, (2, 2)), (1, (2, 2)),
 )
-CHUNKS = ((0, 112), (112, 112), (224, 32))
+CHUNKS = ((0, 96), (96, 96), (192, 64))
 
 
 def nn(a, b):
@@ -431,7 +431,7 @@
 
     def grad_pair(q):
         low, rows = CHUNKS[q]
-        mine, here = pl.ds(al(k * 256 + low, 16), rows), pl.ds(low, rows)
+        mine, here = pl.ds(al(k * 256 + low, 32), rows), pl.ds(low, rows)
 
         @pl.loop(0, NZ)
         def _(zz):
@@ -545,7 +545,7 @@
 
     shift_all(0, 0, 1024, ((0, lambda: layer_second(2)), (1, lambda: grad_y_first(1)), (2, lambda: layer_second(3))))
     grad_y_last(0)
-    shift_all(1, QB, 768, ((0, lambda: layer_second(4)), (2, lambda: layer_second(5))))
+    shift_all(1, QB, 768, ((0, lambda: layer_second(4)), (2, lambda: layer_second(5)), (3, lambda: grad_y_last(1))))
 
     pair_back = rcopy(gks.at[1], gkr.at[1], gs.at[1], gr.at[1], partner)
     far_back = rcopy(gks.at[0], gkr.at[0], gs.at[0], gr.at[0], at_ctx(-2))
@@ -559,7 +559,6 @@
     def _():
         far_back.start()
 
-    grad_y_last(1)
     grad_early_z()
     layer_second(6)
     shift_all(0, 1024, QB, ())
@@ -732,9 +731,9 @@
                 buf(2 * HEADS, 1, QB, kind=F32), buf(2 * HEADS, 1, QB, kind=F32), buf(TOK, TOK),
                 buf(2, HEADS * QB, HEAD), buf(2, HEADS * QB, HEAD),
                 buf(WIN, HEAD, kind=F32), buf(WIN, HEAD, kind=F32),
-                buf(NZ, NY, TOK, 128), buf(NZ, NY, 256, 128), buf(2, NY, NZ, 112, 128),
-                buf(2, 2, 4, 112, 128), buf(2, 2, 2, 4, 112, 128), buf(2, NZ, 112, 128), buf(2, NZ - 1, 112, 128),
-                buf(NZ, NY, 32, 128), buf(NZ - 1, NY, 32, 128), buf(NY, 32, 128), buf(NY - 1, 32, 128),
+                buf(NZ, NY, TOK, 128), buf(NZ, NY, 256, 128), buf(2, NY, NZ, 96, 128),
+                buf(2, 2, 4, 96, 128), buf(2, 2, 2, 4, 96, 128), buf(2, NZ, 96, 128), buf(2, NZ - 1, 96, 128),
+                buf(NZ, NY, 64, 128), buf(NZ - 1, NY, 64, 128), buf(NY, 64, 128), buf(NY - 1, 64, 128),
                 buf(2, 64, 256), buf(64, 256),
                 buf(8, NX, 2, QB, 128), buf(8, 2, QB, 128), buf(8, 2, 2, QB, 128),
                 buf(2, 2, TOK, HEAD), buf(2, 2, TOK, HEAD),

time: 77.5 us -> 71.9 us (0.928)
  Pallas kernels: 76.6 us -> 70.9 us
    pallas_call x1, Pallas kernels: 74.1 us -> 68.3 us  [body(): pl.pallas_call(kernel, out_shape=out_shape, in_specs=[hbm] * 6, out_specs...]
where the time goes in v3:
time: 71.9 us; the launch traced here: 71.7 us
  Pallas kernels  70.9 us (99%)
  between operations  0.8 us (1%)
    pallas_call x1, Pallas kernels, body(): pl.pallas_call(kernel, out_shape=out_shape, in_specs=[hbm] * 6, out_specs...  68.3 us
    pallas_call x1, Pallas kernels, body(): pl.pallas_call(finish, out_shape=out_shape, in_specs=[hbm] * 5, out_specs...  2.55 us

profile of v3, /device:TPU:1, one launch (start us, length us, event | category | flops | bytes accessed | tf_op | source)
XLA Modules:
  0.0 71.7 jit_solution(9175680091920762720)
XLA Ops:
  0.6 68.3 %shard_map.101 = (bf16[512,1024]{1,0:T(8,128)(2,1)}, bf16[512,512]{1,0:T(8,128)(2,1)}, bf16[512,128]{1,0:T(8,128)(2,1)}, bf16[512,128]{1,0:T(8,128)(2,1)}, bf16[64,512]{1,0:T(8,128)(2,1)}) custom-call(s32[1,512]{1,0:T(1,128)} %bitcast.1, bf16[512,512]{1,0:T(8,128)(2,1)} %q_hbm.1, bf16[512,128]{1,0:T(8,128)(2,1)} %k_hbm.1, bf16[512,128]{1,0:T(8,128)(2,1)} %v_hbm.1, ...), custom_call_target="tpu_custom_call" | custom-call | tf_op jit(solution)/shard_map/pallas_call | solution.py:720
  69.0 2.5 %shard_map.102 = (bf16[512,1024]{1,0:T(8,128)(2,1)}, bf16[512,512]{1,0:T(8,128)(2,1)}, bf16[512,128]{1,0:T(8,128)(2,1)}, bf16[512,128]{1,0:T(8,128)(2,1)}, bf16[64,512]{1,0:T(8,128)(2,1)}) custom-call(bf16[512,1024]{1,0:T(8,128)(2,1)} %get-tuple-element.10.refs_0_, bf16[512,512]{1,0:T(8,128)(2,1)} %get-tuple-element.11.refs_1_, ...), custom_call_target="tpu_custom_call" | custom-call | tf_op jit(solution)/shard_map/pallas_call | solution.py:752
